TPU v7x, 512 devices: a whole 4x8x8 slice. The times are simulated.
512 devices in a mesh: team: 32 (over x_hi, y, core), rep: 16 (over x_lo, z).
Axes of the slice: x: 4 (x_hi: 2, x_lo: 2; x = x_hi * 2 + x_lo), y: 8, z: 8, core: 2. Of those that a mesh axis runs over, the one named last changes fastest.
Arguments:
- points: bfloat16 [32768, 128], P('team'), may hold values from -3 to 3
Outputs:
- potential: float32 [32768], P('team')
- displacement: float32 [32768, 128], P('team')
All inputs are finite; a program needn't handle non-finite values.
Results may differ from a plain program's by a relative error of at most 0.0097.
The roundings to bfloat16 on the way count: a program that leaves them out, or rounds other values in their place, can miss the bound.
Values may be sent and summed in bfloat16 or wider, within the bound.
A program may use at most 64 MiB of HBM per device.

v0:
```python
import jax
import jax.numpy as jnp
from jax import lax
from jax.sharding import PartitionSpec as P


def shards(points):
    rows, width = points.shape
    replicas = lax.axis_size("rep")
    teams = lax.axis_size("team")
    part = rows // replicas
    replica = lax.axis_index("rep")
    log_count = jnp.log(jnp.float32(rows * teams))
    mine = lax.dynamic_slice_in_dim(points, replica * part, part, 0)
    cols = lax.all_gather(mine, "team", axis=0, tiled=True)
    half_rows = 0.5 * jnp.sum(jnp.square(points.astype(jnp.float32)), axis=1)
    half_cols = 0.5 * jnp.sum(jnp.square(cols.astype(jnp.float32)), axis=1)
    products = lax.dot_general(
        points, cols, (((1,), (1,)), ((), ())), preferred_element_type=jnp.float32
    )
    cost = half_rows[:, None] + half_cols[None, :] - products
    first = lax.psum(jnp.sum(jnp.exp(cost * -0.25), axis=1), "rep")
    pot_one = -2.0 * (jnp.log(first) - log_count)
    pot_mine = lax.dynamic_slice_in_dim(pot_one, replica * part, part, 0)
    pot_cols = lax.all_gather(pot_mine, "team", axis=0, tiled=True)
    kernel = jnp.exp((pot_cols[None, :] - cost) * 0.5)
    second_part = jnp.sum(kernel, axis=1)
    numer_part = jnp.dot(kernel.astype(jnp.bfloat16), cols, preferred_element_type=jnp.float32)
    second, numer = lax.psum((second_part, numer_part), "rep")
    potential = 0.5 * (pot_one - 2.0 * (jnp.log(second) - log_count))
    displacement = points.astype(jnp.float32) - numer / second[:, None]
    return (potential, displacement)


def solution(mesh):
    return jax.shard_map(
        shards,
        mesh=mesh,
        in_specs=(P("team", None),),
        out_specs=(P("team"), P("team", None)),
        check_vma=False,
    )
```

profile of v0, /device:TPU:8, one launch (start us, length us, event | category | flops | bytes accessed | tf_op | source)
XLA Modules:
  0.0 313.4 jit_solution(10755890835442421011)
XLA Ops:
  7.2 0.0 all-reduce.3.cloned.1.call-start
  7.2 1.2 fusion.4
  8.4 0.7 constant_dynamic-slice_fusion
  9.1 43.6 %all_gather.6 = bf16[2048,128]{1,0:T(8,128)(2,1)S(1)} all-gather(bf16[64,128]{1,0:T(8,128)(2,1)S(1)} %constant_dynamic-slice_fusion), channel_id=1, replica_groups=mesh['team'=32,'rep'=16] {'team'}, dimensions={0}, use_global_device_ids=true | all-gather | bytes 540672 | tf_op jit(solution)/shard_map/all_gather | solution.py:15
  52.7 0.3 multiply_reduce_fusion
  53.0 5.1 %exponential_reduce_fusion = (f32[1024]{0:T(1024)S(1)}, f32[2048,1024]{1,0:T(8,128)}) fusion(f32[2048]{0:T(1024)S(1)} %broadcast_multiply_fusion, f32[1024]{0:T(1024)S(1)} %broadcast_multiply_fusion.1, bf16[2048,128]{1,0:T(8,128)(2,1)S(1)} %all_gather.6, bf16[1024,128]{1,0:T(8,128)(2,1)} %param.1), kind=kOutput, calls=%fused_computation.2 | convolution fusion | flops 545258496 | bytes 9191424 | tf_op jit(solution)/shard_map/dot_general | solution.py:18
  58.1 36.0 %psum.21 = f32[1024]{0:T(1024)S(1)} all-reduce(f32[1024]{0:T(1024)S(1)} %get-tuple-element.2), channel_id=1, replica_groups=mesh['team'=32,'rep'=16] {'rep'}, use_global_device_ids=true, to_apply=%region_3.0 | all-reduce | flops 1024 | bytes 8192 | tf_op jit(solution)/shard_map/psum | solution.py:22
  94.1 1.3 dynamic-slice
  96.0 0.2 dynamic-slice_dynamic-update-slice_fusion
  96.2 64.4 %all-reduce = f32[2048]{0:T(1024)S(1)} all-reduce(f32[2048]{0:T(1024)S(1)} %dynamic-slice_dynamic-update-slice_fusion), channel_id=1, replica_groups=mesh['team'=32,'rep'=16] {'team'}, use_global_device_ids=true, to_apply=%add | all-reduce | flops 2048 | bytes 16384
  160.6 5.5 %fusion.2 = f32[1024,128]{1,0:T(8,128)} fusion(bf16[2048,128]{1,0:T(8,128)(2,1)S(1)} %all_gather.6, f32[2048,1024]{1,0:T(8,128)} %get-tuple-element.3, f32[2048]{0:T(1024)S(1)} %all-reduce, f32[2048]{0:T(1024)S(1)} %broadcast_multiply_fusion, f32[1024]{0:T(1024)S(1)} %broadcast_multiply_fusion.1), kind=kOutput, calls=%fused_computation.5 | convolution fusion | flops 547356672 | bytes 9457664 | tf_op jit(solution)/shard_map/dot_general | solution.py:28
  166.1 0.0 copy-start
  166.1 0.0 all-reduce.3.cloned.1.call-update
  166.2 4.5 %fusion.1 = f32[1024]{0:T(1024)S(1)} fusion(f32[2048,1024]{1,0:T(8,128)} %get-tuple-element.3, f32[2048]{0:T(1024)S(1)} %all-reduce, f32[2048]{0:T(1024)S(1)} %broadcast_multiply_fusion, f32[1024]{0:T(1024)S(1)} %broadcast_multiply_fusion.1), kind=kLoop, calls=%fused_computation.4 | loop fusion | flops 10484736 | bytes 8413184 | tf_op jit(solution)/shard_map/reduce_sum | solution.py:27
  170.7 30.6 %psum.22 = f32[1024]{0:T(1024)S(1)} all-reduce(f32[1024]{0:T(1024)S(1)} %fusion.1), channel_id=1, replica_groups=mesh['team'=32,'rep'=16] {'rep'}, use_global_device_ids=true, to_apply=%region_5.0 | all-reduce | flops 1024 | bytes 8192 | tf_op jit(solution)/shard_map/psum | solution.py:29
  201.3 0.6 subtract_multiply_fusion
  202.0 102.5 %all-reduce.3.cloned.1.call-done = f32[1024,128]{1,0:T(8,128)} async-done(((f32[1024,128]{1,0:T(8,128)}), f32[1024,128]{1,0:T(8,128)}) %all-reduce.3.cloned.1.call-update) | async-done | bytes 524304 | tf_op jit(solution)/shard_map/psum | solution.py:29
  304.5 0.0 copy-done
  304.5 2.0 convert_subtract_fusion
  (4 shorter events, 0.0 us)
Async XLA Ops:
  7.2 297.3 %all-reduce.3.cloned.1.call-start = ((), (), s32[]{:S(2)}) async-start(), calls=%async_computation | async-start | bytes 1048576 | tf_op jit(solution)/shard_map/psum | solution.py:29
  166.1 138.3 %copy-start = (bf16[1024,128]{1,0:T(8,128)(2,1)S(1)}, bf16[1024,128]{1,0:T(8,128)(2,1)}, u32[]{:S(2)}) copy-start(bf16[1024,128]{1,0:T(8,128)(2,1)} %param.1) | copy-start | bytes 786436
Sparse Core Ops, SparseCore 0:
  166.3 138.1 all-reduce.2
where the time goes:
time: 314 us; the launch traced here: 313 us
  blocking collectives  175 us (56%)
  waiting for transfers between devices  103 us (33%)
  between operations  14.7 us (5%)
  matrix products  10.6 us (3%)
  other arithmetic  8.71 us (3%)
    psum x1, waiting for transfers between devices, shards(): second, numer = lax.psum((second_part, numer_part), 'rep')  103 us
    unnamed x1, blocking collectives  64.4 us
    all_gather x1, blocking collectives, shards(): cols = lax.all_gather(mine, 'team', axis=0, tiled=True)  43.6 us
    psum x1, blocking collectives, shards(): first = lax.psum(jnp.sum(jnp.exp(cost * -0.25), axis=1), 'rep')  36 us
    psum x1, blocking collectives, shards(): second, numer = lax.psum((second_part, numer_part), 'rep')  30.6 us
  transfers between devices with their start and end apart: 1, of which 1 were waited for; matrix products, arithmetic and copies ran while one was open for 2% of the time, Pallas kernels for 0%

commit v1 on v0

--- a/solution.py
+++ b/solution.py
@@ -12,7 +12,8 @@
     replica = lax.axis_index("rep")
     log_count = jnp.log(jnp.float32(rows * teams))
     mine = lax.dynamic_slice_in_dim(points, replica * part, part, 0)
-    cols = lax.all_gather(mine, "team", axis=0, tiled=True)
+    sent = jnp.stack([mine] * lax.axis_size("team"))
+    cols = jnp.concatenate(lax.all_to_all(sent, "team", 0, 0), axis=0)
     half_rows = 0.5 * jnp.sum(jnp.square(points.astype(jnp.float32)), axis=1)
     half_cols = 0.5 * jnp.sum(jnp.square(cols.astype(jnp.float32)), axis=1)
     products = lax.dot_general(

time: 314 us -> 297 us (0.946)
  blocking collectives: 175 us -> 131 us
  waiting for transfers between devices: 103 us -> 118 us
  starting transfers between devices: 0.04 us -> 10.2 us
    all_gather x1 -> x0, blocking collectives: 43.6 us -> none  [shards(): cols = lax.all_gather(mine, 'team', axis=0, tiled=True)]
    all_to_all x0 -> x1, waiting for transfers between devices: none -> 16.1 us  [shards(): cols = jnp.concatenate(lax.all_to_all(sent, 'team', 0, 0), axis=0)]
    all_to_all x0 -> x1, starting transfers between devices: none -> 10.2 us  [shards(): cols = jnp.concatenate(lax.all_to_all(sent, 'team', 0, 0), axis=0)]
    psum x1, blocking collectives: 36 us -> 39.7 us  [shards(): first = lax.psum(jnp.sum(jnp.exp(cost * -0.25), axis=1), 'rep')]
    unnamed x1, blocking collectives: 64.4 us -> 61 us
  transfers between devices with their start and end apart: 1 -> 2, of which waited for: 1 -> 2; matrix products, arithmetic and copies ran while one was open for 2% -> 3% of each run, Pallas kernels for 0% -> 0%
where the time goes in v1:
time: 297 us
  blocking collectives  131 us (44%)
  waiting for transfers between devices  118 us (40%)
  between operations  14.7 us (5%)
  matrix products  10.6 us (4%)
  starting transfers between devices  10.2 us (3%)
  other arithmetic  8.71 us (3%)
  local copies, waits for them, and re-layouts  3.18 us (1%)
    psum x1, waiting for transfers between devices, shards(): second, numer = lax.psum((second_part, numer_part), 'rep')  102 us
    unnamed x1, blocking collectives  61 us
    psum x1, blocking collectives, shards(): first = lax.psum(jnp.sum(jnp.exp(cost * -0.25), axis=1), 'rep')  39.7 us
    psum x1, blocking collectives, shards(): second, numer = lax.psum((second_part, numer_part), 'rep')  30.6 us
    all_to_all x1, waiting for transfers between devices, shards(): cols = jnp.concatenate(lax.all_to_all(sent, 'team', 0, 0), axis=0)  16.1 us
    all_to_all x1, starting transfers between devices, shards(): cols = jnp.concatenate(lax.all_to_all(sent, 'team', 0, 0), axis=0)  10.2 us
  transfers between devices with their start and end apart: 2, of which 2 were waited for; matrix products, arithmetic and copies ran while one was open for 3% of the time, Pallas kernels for 0%

profile of v1, /device:TPU:8, one launch (start us, length us, event | category | flops | bytes accessed | tf_op | source)
XLA Modules:
  0.0 296.8 jit_solution(2645927778041121230)
XLA Ops:
  7.2 0.7 constant_dynamic-slice_fusion
  7.9 0.9 stack.2
  8.8 10.2 %all-to-all-start = ((bf16[32,64,128]{2,1,0:T(8,128)(2,1)}), bf16[32,64,128]{2,1,0:T(8,128)(2,1)S(1)}, u32[]{:S(2)}, u32[]{:S(2)}) async-start(bf16[32,64,128]{2,1,0:T(8,128)(2,1)} %stack.2), calls=%async_computation | async-start | bytes 1048576 | tf_op jit(solution)/shard_map/all_to_all | solution.py:16
  19.0 0.0 all-reduce.3.cloned.1.call-start
  19.0 1.3 dynamic-slice
  21.0 1.2 fusion.4
  22.1 16.1 %all-to-all-done = bf16[32,64,128]{2,1,0:T(8,128)(2,1)S(1)} async-done(((bf16[32,64,128]{2,1,0:T(8,128)(2,1)}), bf16[32,64,128]{2,1,0:T(8,128)(2,1)S(1)}, u32[]{:S(2)}, u32[]{:S(2)}) %all-to-all-start) | async-done | bytes 524320 | tf_op jit(solution)/shard_map/all_to_all | solution.py:16
  38.2 0.3 multiply_reduce_fusion
  38.6 0.1 mul.55
  38.6 5.1 %exponential_reduce_fusion = (f32[1024]{0:T(1024)S(1)}, f32[2048,1024]{1,0:T(8,128)}) fusion(f32[2048]{0:T(1024)S(1)} %mul.55, f32[1024]{0:T(1024)S(1)} %broadcast_multiply_fusion.1, bf16[2048,128]{1,0:T(8,128)(2,1)S(1)} %bitcast.16, bf16[1024,128]{1,0:T(8,128)(2,1)} %param.1), kind=kOutput, calls=%fused_computation.2 | convolution fusion | flops 545258496 | bytes 9191424 | tf_op jit(solution)/shard_map/dot_general | solution.py:19
  43.7 39.7 %psum.21 = f32[1024]{0:T(1024)S(1)} all-reduce(f32[1024]{0:T(1024)S(1)} %get-tuple-element.2), channel_id=1, replica_groups=mesh['team'=32,'rep'=16] {'rep'}, use_global_device_ids=true, to_apply=%region_3.0 | all-reduce | flops 1024 | bytes 8192 | tf_op jit(solution)/shard_map/psum | solution.py:23
  83.4 0.2 dynamic-slice_dynamic-update-slice_fusion
  83.6 61.0 %all-reduce = f32[2048]{0:T(1024)S(1)} all-reduce(f32[2048]{0:T(1024)S(1)} %dynamic-slice_dynamic-update-slice_fusion), channel_id=1, replica_groups=mesh['team'=32,'rep'=16] {'team'}, use_global_device_ids=true, to_apply=%add | all-reduce | flops 2048 | bytes 16384
  144.6 5.5 %fusion.2 = f32[1024,128]{1,0:T(8,128)} fusion(bf16[2048,128]{1,0:T(8,128)(2,1)S(1)} %bitcast.17, f32[2048,1024]{1,0:T(8,128)} %get-tuple-element.3, f32[2048]{0:T(1024)S(1)} %all-reduce, f32[2048]{0:T(1024)S(1)} %mul.55, f32[1024]{0:T(1024)S(1)} %broadcast_multiply_fusion.1), kind=kOutput, calls=%fused_computation.5 | convolution fusion | flops 547356672 | bytes 9457664 | tf_op jit(solution)/shard_map/dot_general | solution.py:29
  150.1 0.0 copy-start
  150.1 0.0 all-reduce.3.cloned.1.call-update
  150.2 4.5 %fusion.1 = f32[1024]{0:T(1024)S(1)} fusion(f32[2048,1024]{1,0:T(8,128)} %get-tuple-element.3, f32[2048]{0:T(1024)S(1)} %all-reduce, f32[2048]{0:T(1024)S(1)} %mul.55, f32[1024]{0:T(1024)S(1)} %broadcast_multiply_fusion.1), kind=kLoop, calls=%fused_computation.4 | loop fusion | flops 10484736 | bytes 8413184 | tf_op jit(solution)/shard_map/reduce_sum | solution.py:28
  154.7 30.6 %psum.22 = f32[1024]{0:T(1024)S(1)} all-reduce(f32[1024]{0:T(1024)S(1)} %fusion.1), channel_id=1, replica_groups=mesh['team'=32,'rep'=16] {'rep'}, use_global_device_ids=true, to_apply=%region_5.0 | all-reduce | flops 1024 | bytes 8192 | tf_op jit(solution)/shard_map/psum | solution.py:30
  185.3 0.6 subtract_multiply_fusion
  185.9 101.9 %all-reduce.3.cloned.1.call-done = f32[1024,128]{1,0:T(8,128)} async-done(((f32[1024,128]{1,0:T(8,128)}), f32[1024,128]{1,0:T(8,128)}) %all-reduce.3.cloned.1.call-update) | async-done | bytes 524304 | tf_op jit(solution)/shard_map/psum | solution.py:30
  287.9 0.0 copy-done
  287.9 2.0 convert_subtract_fusion
  (4 shorter events, 0.0 us)
Async XLA Ops:
  8.8 29.4 %all-to-all-start = ((bf16[32,64,128]{2,1,0:T(8,128)(2,1)}), bf16[32,64,128]{2,1,0:T(8,128)(2,1)S(1)}, u32[]{:S(2)}, u32[]{:S(2)}) async-start(bf16[32,64,128]{2,1,0:T(8,128)(2,1)} %stack.2), calls=%async_computation | async-start | bytes 1048576 | tf_op jit(solution)/shard_map/all_to_all | solution.py:16
  19.0 268.9 %all-reduce.3.cloned.1.call-start = ((), (), s32[]{:S(2)}) async-start(), calls=%async_computation.1 | async-start | bytes 1048576 | tf_op jit(solution)/shard_map/psum | solution.py:30
  150.1 137.7 %copy-start = (bf16[1024,128]{1,0:T(8,128)(2,1)S(1)}, bf16[1024,128]{1,0:T(8,128)(2,1)}, u32[]{:S(2)}) copy-start(bf16[1024,128]{1,0:T(8,128)(2,1)} %param.1) | copy-start | bytes 786436
Sparse Core Ops, SparseCore 0:
  150.3 137.5 all-reduce.2
